TPU v7x, 512 devices: a whole 4x4x16 slice. The times are simulated.
512 devices in a mesh: dp: 8 (over x, y_lo), tm: 64 (over z, y_hi, core).
Axes of the slice: x: 4, y: 4 (y_hi: 2, y_lo: 2; y = y_hi * 2 + y_lo), z: 16, core: 2. Of those that a mesh axis runs over, the one named last changes fastest.
Arguments:
- features: bfloat16 [8, 8192, 1536], P('dp', 'tm'), may hold values from -8 to 8
- start_noise: bfloat16 [8, 8192, 1536], P('dp', 'tm'), may hold values from -1 to 1
- cotangent: bfloat16 [8, 8192, 1536], P('dp', 'tm'), may hold values from -0.0234375 to 0.0234375
- in_weight: bfloat16 [3072, 1536], P('tm'), may hold values from -0.15625 to 0.15625
- kernel: float32 [31, 1536], replicated, may hold values from -1 to 1
- bn_gain: float32 [1536], replicated, may hold values from 0.25 to 1.75
- bn_shift: float32 [1536], replicated, may hold values from -1 to 1
- ends: int32 [8], replicated, may hold values from 4096 to 8192
Outputs:
- perturbation: float32 [8, 8192, 1536], P('dp', 'tm')
- grad_kernel: float32 [31, 1536], P(None, 'tm')
- grad_norm: float32 [2, 1536], P(None, 'tm')
Inputs may be any that keep to these rules, and one draw needn't show every extreme that they name: `ends`: frames at or after an utterance's end are padding.
All inputs are finite; a program needn't handle non-finite values.
Results may differ from a plain program's by a relative error of at most 0.0059.
Values may be sent and summed in bfloat16 or wider, within the bound.
A program may use at most 128 MiB of HBM per device.

v0:
```python
import jax
import jax.numpy as jnp
from jax import lax
from jax.sharding import PartitionSpec as P

ASCENT = 2
noise_scale = 0.5
ascent_rate = 0.5
layer_epsilon = 1e-05
batch_epsilon = 1e-05
ascent_epsilon = 1e-06


def normalize(summed):
    centre = summed - jnp.mean(summed, axis=-1, keepdims=True)
    inverse = lax.rsqrt(jnp.mean(centre * centre, axis=-1, keepdims=True) + layer_epsilon)
    return (centre * inverse, inverse)


def with_halo(block, half_span):
    count = lax.axis_size("tm")
    before = lax.ppermute(block[-half_span:], "tm", [(i, i + 1) for i in range(count - 1)])
    after = lax.ppermute(block[:half_span], "tm", [(i + 1, i) for i in range(count - 1)])
    return jnp.concatenate([before, block, after], axis=0).astype(jnp.float32)


def conv(padded, kernel, out_length, flip):
    taps = kernel.shape[0]
    result = None
    for offset in range(taps):
        start = taps - 1 - offset if flip else offset
        term = kernel[offset] * padded[start : start + out_length]
        result = term if result is None else result + term
    return result


def tap_grad(grad, padded, taps):
    rows = grad.shape[0]
    return jnp.stack([jnp.sum(grad * padded[j : j + rows], axis=0) for j in range(taps)])


def on_device(features, start_noise, cotangent, in_weight, kernel, bn_gain, bn_shift, ends):
    frame_rows = features.shape[1]
    model_width = features.shape[2]
    tap_count = kernel.shape[0]
    half_span = (tap_count - 1) // 2
    shard_index = lax.axis_index("tm")
    group_index = lax.axis_index("dp")
    utter_end = lax.dynamic_index_in_dim(ends, group_index, 0, keepdims=False)
    live_count = jnp.sum(ends).astype(jnp.float32)
    utter_length = utter_end.astype(jnp.float32)
    frame_ids = shard_index * frame_rows + jnp.arange(frame_rows, dtype=jnp.int32)
    live = (frame_ids < utter_end).astype(jnp.float32)[:, None]
    weight_full = lax.all_gather(in_weight, "tm", axis=0, tiled=True)
    inputs = features[0].astype(jnp.float32)
    perturbation = noise_scale * start_noise[0].astype(jnp.float32) * live
    upstream = live * cotangent[0].astype(jnp.float32) / ASCENT
    everywhere = ("dp", "tm")
    kernel_part = 0.0
    norm_part = 0.0
    for ascent_step in range(ASCENT):
        summed = inputs + perturbation
        normed, inverse = normalize(summed)
        hidden = lax.dot_general(
            normed.astype(jnp.bfloat16),
            weight_full,
            (((1,), (1,)), ((), ())),
            preferred_element_type=jnp.float32,
        )
        value_half = hidden[:, :model_width]
        gate_half = jax.nn.sigmoid(hidden[:, model_width:])
        glu = (value_half * gate_half * live).astype(jnp.bfloat16)
        padded = with_halo(glu, half_span)
        conv_out = conv(padded, kernel, frame_rows, False)
        batch_mean = lax.psum(jnp.sum(live * conv_out, axis=0), everywhere) / live_count
        centred = conv_out - batch_mean
        variance = lax.psum(jnp.sum(live * centred * centred, axis=0), everywhere) / live_count
        inv_std = lax.rsqrt(variance + batch_epsilon)
        scaled = centred * inv_std
        pre_act = bn_gain * scaled + bn_shift
        pre_sigmoid = jax.nn.sigmoid(pre_act)
        grad_pre = upstream * pre_sigmoid * (1.0 + pre_act * (1.0 - pre_sigmoid))
        both = lax.psum(
            jnp.stack([jnp.sum(grad_pre * scaled, axis=0), jnp.sum(grad_pre, axis=0)]), everywhere
        )
        norm_part = norm_part + both
        grad_conv = (
            live * inv_std * bn_gain * (grad_pre - (both[1] + scaled * both[0]) / live_count)
        ).astype(jnp.bfloat16)
        kernel_part = kernel_part + tap_grad(grad_conv.astype(jnp.float32), padded, tap_count)
        if ascent_step + 1 < ASCENT:
            grad_pad = with_halo(grad_conv, half_span)
            grad_glu = (conv(grad_pad, kernel, frame_rows, True) * live).astype(jnp.bfloat16)
            grad_float = grad_glu.astype(jnp.float32)
            grad_hidden = jnp.concatenate(
                [grad_float * gate_half, grad_float * value_half * gate_half * (1.0 - gate_half)],
                axis=1,
            ).astype(jnp.bfloat16)
            grad_normed = jnp.dot(grad_hidden, weight_full, preferred_element_type=jnp.float32)
            direction = (
                live
                * inverse
                * (
                    grad_normed
                    - jnp.mean(grad_normed, axis=-1, keepdims=True)
                    - normed * jnp.mean(grad_normed * normed, axis=-1, keepdims=True)
                )
            )
            square_total = lax.psum(jnp.sum(direction * direction), "tm")
            perturbation = perturbation + direction * (
                ascent_rate
                * jnp.sqrt(utter_length * model_width)
                / (jnp.sqrt(square_total) + ascent_epsilon)
            )
    width = model_width // lax.axis_size("tm")
    by_shard = jnp.transpose(kernel_part.reshape(tap_count, -1, width), (1, 0, 2))
    by_shard = jnp.pad(by_shard.reshape(by_shard.shape[0], -1), ((0, 0), (0, 24)))
    kernel_total = lax.psum_scatter(by_shard.reshape(-1, 6, 128), "tm", scatter_dimension=0)
    kernel_total = lax.psum(kernel_total, "dp").reshape(-1)[: tap_count * width]
    kernel_total = kernel_total.reshape(tap_count, width)
    norm_total = lax.dynamic_slice_in_dim(norm_part, shard_index * width, width, 1)
    return (perturbation[None], kernel_total, norm_total)


def solution(mesh):
    return jax.shard_map(
        on_device,
        mesh=mesh,
        in_specs=(
            P("dp", "tm", None),
            P("dp", "tm", None),
            P("dp", "tm", None),
            P("tm", None),
            P(),
            P(),
            P(),
            P(),
        ),
        out_specs=(P("dp", "tm", None), P(None, "tm"), P(None, "tm")),
        check_vma=False,
    )
```

profile of v0, /device:TPU:2, one launch (start us, length us, event | category | flops | bytes accessed | tf_op | source)
XLA Modules:
  0.0 1536.4 jit_solution(2124826723035073364)
XLA Ops:
  7.2 0.7 all-gather.2.cloned.1.call-update
  8.0 1.2 dynamic_slice.7
  9.2 0.6 fusion.133
  9.9 0.7 broadcast_select_fusion.1
  10.6 1.7 slice_reduce_fusion.34
  12.3 1.4 fusion.121
  13.7 1.4 multiply_reduce_fusion.7
  15.1 1.2 broadcast_select_fusion
  16.3 168.6 %all-gather.2.cloned.1.call-done = bf16[3072,1536]{1,0:T(8,128)(2,1)} async-done(((bf16[48,1536]{1,0:T(8,128)(2,1)}), bf16[3072,1536]{1,0:T(8,128)(2,1)}) %all-gather.2.cloned.1.call-update) | async-done | bytes 9437200 | tf_op jit(solution)/shard_map/all_gather | solution.py:54
  184.9 6.9 fusion.122
  191.9 0.2 multiply_convert_fusion.3
  192.1 2.2 collective-permute-start
  194.3 1.3 collective-permute-start.1
  195.6 2.0 slice_reduce_fusion.33
  197.6 0.6 reduce_sum.705
  199.6 0.1 maximum_convert_fusion
  199.8 4.6 multiply_reduce_fusion.6
  204.3 104.9 %psum.56 = f32[1536]{0:T(1024)} all-reduce(f32[1536]{0:T(1024)} %get-tuple-element.124), channel_id=1, replica_groups=mesh['dp'=8,'tm'=64] {'dp','tm'}, use_global_device_ids=true, to_apply=%region_3.4 | all-reduce | flops 1536 | bytes 12288 | tf_op jit(solution)/shard_map/psum | solution.py:75
  309.2 0.7 broadcast_divide_fusion.1
  309.9 1.4 fusion.4
  311.3 99.4 %psum.57 = f32[1536]{0:T(1024)} all-reduce(f32[1536]{0:T(1024)} %fusion.4), channel_id=1, replica_groups=mesh['dp'=8,'tm'=64] {'dp','tm'}, use_global_device_ids=true, to_apply=%region_6.7 | all-reduce | flops 1536 | bytes 12288 | tf_op jit(solution)/shard_map/psum | solution.py:77
  410.7 0.7 add_rsqrt_fusion.1
  411.4 0.6 copy-done.21
  412.0 2.4 multiply_reduce_fusion.5
  414.4 0.6 pad_maximum_fusion
  415.0 100.9 %psum.58 = f32[2,1536]{1,0:T(2,128)} all-reduce(f32[2,1536]{1,0:T(2,128)} %pad_maximum_fusion), channel_id=1, replica_groups=mesh['dp'=8,'tm'=64] {'dp','tm'}, use_global_device_ids=true, to_apply=%region_9.10 | all-reduce | flops 3072 | bytes 24576 | tf_op jit(solution)/shard_map/psum | solution.py:83
  515.9 0.8 slice_reduce_fusion.3
  516.7 4.1 fusion.36
  520.9 1.2 fusion.35
  522.3 0.1 stack.214
  527.2 1.8 collective-permute-start.2
  528.9 1.3 collective-permute-start.3
  530.7 3.2 collective-permute-done.3
  534.0 0.1 maximum_convert_fusion.1
  534.2 3.2 fusion
  537.5 0.3 fusion.3
  537.8 0.7 copy-done.1
  538.5 0.1 copy-done.3
  538.7 1.5 fusion.134
  540.2 1.2 multiply_reduce_fusion.3
  541.4 133.6 %psum.59 = f32[]{:T(128)} all-reduce(f32[]{:T(128)} %get-tuple-element.119), channel_id=1, replica_groups=mesh['dp'=8,'tm'=64] {'tm'}, use_global_device_ids=true, to_apply=%region_13.14 | all-reduce | flops 1 | bytes 8 | tf_op jit(solution)/shard_map/psum | solution.py:109
  675.7 1.1 fusion.136
  676.9 0.2 multiply_reduce_fusion.2
  677.1 6.8 fusion.124
  684.0 0.2 fusion.118
  684.2 1.3 collective-permute-start.4
  685.5 1.5 collective-permute-start.5
  687.1 1.6 collective-permute-done.5
  688.6 0.1 maximum_convert_fusion.2
  688.8 3.1 multiply_reduce_fusion.1
  692.0 114.4 %psum.60 = f32[1536]{0:T(1024)S(1)} all-reduce(f32[1536]{0:T(1024)S(1)} %get-tuple-element.114), channel_id=1, replica_groups=mesh['dp'=8,'tm'=64] {'dp','tm'}, use_global_device_ids=true, to_apply=%region_48.49 | all-reduce | flops 1536 | bytes 12288 | tf_op jit(solution)/shard_map/psum | solution.py:75
  806.4 0.2 fusion.5
  806.6 99.4 %psum.61 = f32[1536]{0:T(1024)S(1)} all-reduce(f32[1536]{0:T(1024)S(1)} %fusion.5), channel_id=1, replica_groups=mesh['dp'=8,'tm'=64] {'dp','tm'}, use_global_device_ids=true, to_apply=%region_50.51 | all-reduce | flops 1536 | bytes 12288 | tf_op jit(solution)/shard_map/psum | solution.py:77
  906.0 1.2 multiply_reduce_fusion
  907.3 100.4 %psum.62 = f32[2,1536]{1,0:T(2,128)S(1)} all-reduce(f32[2,1536]{1,0:T(2,128)S(1)} %pad_maximum_fusion.1), channel_id=1, replica_groups=mesh['dp'=8,'tm'=64] {'dp','tm'}, use_global_device_ids=true, to_apply=%region_53.54 | all-reduce | flops 3072 | bytes 24576 | tf_op jit(solution)/shard_map/psum | solution.py:83
  1007.8 2.3 fusion.67
  1010.1 1.2 fusion.66
  1016.8 0.9 copy.78
  1017.7 1.4 dynamic-slice
  1019.0 1.3 dynamic-slice_add_fusion
  1020.4 475.1 %all-reduce.4.cloned.1.call-done = f32[64,6,128]{2,1,0:T(8,128)} async-done(((f32[64,6,128]{2,1,0:T(8,128)}), f32[64,6,128]{2,1,0:T(8,128)}) %all-reduce.4.cloned.1.call-update) | async-done | bytes 196624
  1495.5 1.4 constant_dynamic-slice_fusion
  1496.9 32.0 %psum.63 = f32[32,24]{1,0:T(8,128)S(1)} all-reduce(f32[32,24]{1,0:T(8,128)S(1)} %slice.682), channel_id=1, replica_groups=mesh['dp'=8,'tm'=64] {'dp'}, use_global_device_ids=true, to_apply=%region_86.87 | all-reduce | flops 768 | bytes 6144 | tf_op jit(solution)/shard_map/psum | solution.py:119
  1528.9 0.7 copy.77
  (314 shorter events, 10.4 us)
Async XLA Ops:
  7.2 177.8 %copy-start = (bf16[1,128,1536]{2,1,0:T(8,128)(2,1)S(1)}, bf16[1,128,1536]{2,1,0:T(8,128)(2,1)}, u32[]{:S(2)}) copy-start(bf16[1,128,1536]{2,1,0:T(8,128)(2,1)} %param.9) | copy-start | bytes 1179652
  7.2 177.7 %copy-start.2 = (bf16[1,128,1536]{2,1,0:T(8,128)(2,1)S(1)}, bf16[1,128,1536]{2,1,0:T(8,128)(2,1)}, u32[]{:S(2)}) copy-start(bf16[1,128,1536]{2,1,0:T(8,128)(2,1)} %param.8) | copy-start | bytes 1179652
  7.2 177.7 %all-gather.2.cloned.1.call-start = ((), (), s32[]{:S(2)}) async-start(), calls=%async_computation | async-start | bytes 9584640 | tf_op jit(solution)/shard_map/all_gather | solution.py:54
  7.9 1487.5 %all-reduce.4.cloned.1.call-start = ((), (), s32[]{:S(2)}) async-start(), calls=%async_computation.1 | async-start | bytes 524288
  9.9 182.0 %copy-start.22 = (f32[128]{0:T(128)}, f32[128]{0:T(128)S(1)}, u32[]{:S(2)}) copy-start(f32[128]{0:T(128)S(1)} %fusion.133) | copy-start | bytes 1540
  10.5 181.3 %copy-start.42 = (f32[128]{0:T(128)}, f32[128]{0:T(128)S(1)}, u32[]{:S(2)}) copy-start(f32[128]{0:T(128)S(1)} %broadcast_select_fusion.1) | copy-start | bytes 1540
  13.7 178.2 %copy-start.46 = (f32[128]{0:T(128)}, f32[128]{0:T(128)S(1)}, u32[]{:S(2)}) copy-start(f32[128]{0:T(128)S(1)} %broadcast_multiply_fusion.3) | copy-start | bytes 1540
  16.3 175.5 %copy-start.44 = (f32[128]{0:T(128)}, f32[128]{0:T(128)S(1)}, u32[]{:S(2)}) copy-start(f32[128]{0:T(128)S(1)} %get-tuple-element.134) | copy-start | bytes 1540
  191.9 5.7 copy-start.49
  192.1 7.4 collective-permute-start
  194.3 5.3 collective-permute-start.1
  197.6 6.7 copy-start.8
  199.7 212.3 %copy-start.7 = (f32[1536]{0:T(1024)S(1)}, f32[1536]{0:T(1024)}, u32[]{:S(2)}) copy-start(f32[1536]{0:T(1024)} %param.13) | copy-start | bytes 18436
  411.4 0.6 copy-start.21
  520.8 1.3 copy-start.4
  520.8 1.5 copy-start.41
  520.8 1.7 copy-start.40
  520.8 1.9 copy-start.39
  520.8 2.0 copy-start.38
  520.8 2.2 copy-start.37
  520.8 2.3 copy-start.36
  520.8 2.5 copy-start.35
  520.8 2.7 copy-start.34
  520.8 2.8 copy-start.33
  520.8 3.0 copy-start.32
  520.9 3.1 copy-start.31
  520.9 3.3 copy-start.30
  520.9 3.4 copy-start.29
  520.9 3.6 copy-start.28
  520.9 3.7 copy-start.27
  522.1 2.7 copy-start.26
  522.1 2.9 copy-start.25
  522.6 8.0 copy-start.24
  522.7 11.2 copy-start.5
  525.6 8.6 copy-start.9
  525.6 8.6 copy-start.10
  525.6 8.6 copy-start.11
  525.6 8.6 copy-start.13
  525.6 8.6 copy-start.15
  525.6 8.6 copy-start.17
  525.6 8.6 copy-start.19
  525.6 8.6 copy-start.23
  527.2 3.6 collective-permute-start.2
  528.9 5.0 collective-permute-start.3
  534.0 3.8 slice-start
  534.2 3.6 slice-start.1
  534.2 3.6 slice-start.2
  537.5 1.1 copy-start.1
  537.5 1.2 copy-start.3
  537.5 1.2 copy-start.43
  537.5 1.1 copy-start.45
  537.5 1.1 copy-start.47
  538.7 1.5 copy-start.48
  683.9 4.9 copy-start.12
  683.9 4.9 copy-start.14
  683.9 4.9 copy-start.16
  683.9 4.9 copy-start.18
  683.9 4.9 copy-start.20
  684.2 2.8 collective-permute-start.4
  685.5 3.1 collective-permute-start.5
  688.8 217.2 %copy-start.6 = (bf16[1,128,1536]{2,1,0:T(8,128)(2,1)S(1)}, bf16[1,128,1536]{2,1,0:T(8,128)(2,1)}, u32[]{:S(2)}) copy-start(bf16[1,128,1536]{2,1,0:T(8,128)(2,1)} %param.10) | copy-start | bytes 1179652
Sparse Core Ops, SparseCore 0:
  11.3 173.5 all-gather.1
  1017.8 477.6 all-reduce.3
where the time goes:
time: 1540 us
  blocking collectives  785 us (51%)
  waiting for transfers between devices  649 us (42%)
  other arithmetic  38 us (2%)
  local copies, waits for them, and re-layouts  21.8 us (1%)
  between operations  17.9 us (1%)
    unnamed x3, waiting for transfers between devices  476 us
    psum x2, blocking collectives, on_device(): lax.psum(jnp.sum(live * conv_out, axis=0), everywhere) / live_count  219 us
    psum x2, blocking collectives, on_device(): lax.psum(jnp.stack([jnp.sum(grad_pre * scaled, axis=0), jnp.sum(grad_pre,...  201 us
    psum x2, blocking collectives, on_device(): lax.psum(jnp.sum(live * centred * centred, axis=0), everywhere) / live_count  199 us
    all_gather x1, waiting for transfers between devices, on_device(): weight_full = lax.all_gather(in_weight, 'tm', axis=0, tiled=True)  169 us
    psum x1, blocking collectives, on_device(): square_total = lax.psum(jnp.sum(direction * direction), 'tm')  134 us
    psum x1, blocking collectives, on_device(): kernel_total = lax.psum(kernel_total, 'dp').reshape(-1)[:tap_count * width]  32 us
  transfers between devices with their start and end apart: 8, of which 4 were waited for; matrix products, arithmetic and copies ran while one was open for 1% of the time, Pallas kernels for 0%

commit v1 on v0

--- a/solution.py
+++ b/solution.py
@@ -9,6 +9,12 @@
 layer_epsilon = 1e-05
 batch_epsilon = 1e-05
 ascent_epsilon = 1e-06
+
+
+def summed_here(x, axis):
+    blocks = lax.all_gather(x, axis, axis=0, tiled=False)
+    total = blocks.sum(axis=0)
+    return total
 
 
 def normalize(summed):
@@ -80,7 +86,7 @@
         pre_act = bn_gain * scaled + bn_shift
         pre_sigmoid = jax.nn.sigmoid(pre_act)
         grad_pre = upstream * pre_sigmoid * (1.0 + pre_act * (1.0 - pre_sigmoid))
-        both = lax.psum(
+        both = summed_here(
             jnp.stack([jnp.sum(grad_pre * scaled, axis=0), jnp.sum(grad_pre, axis=0)]), everywhere
         )
         norm_part = norm_part + both

time: 1540 us -> 2970 us (1.93)
  waiting for transfers between devices: 649 us -> 2270 us
  blocking collectives: 785 us -> 576 us
    all_gather x0 -> x2, waiting for transfers between devices: none -> 1630 us  [summed_here(): blocks = lax.all_gather(x, axis, axis=0, tiled=False)]
    psum x2 -> x0, blocking collectives: 201 us -> none  [on_device(): lax.psum(jnp.stack([jnp.sum(grad_pre * scaled, axis=0), jnp.sum(grad_pre,...]
    unnamed x3 -> x5, waiting for transfers between devices: 476 us -> 476 us
  transfers between devices with their start and end apart: 8 -> 10, of which waited for: 4 -> 5; matrix products, arithmetic and copies ran while one was open for 1% -> 1% of each run, Pallas kernels for 0% -> 0%
where the time goes in v1:
time: 2970 us
  waiting for transfers between devices  2270 us (76%)
  blocking collectives  576 us (19%)
  other arithmetic  54.1 us (2%)
    all_gather x2, waiting for transfers between devices, summed_here(): blocks = lax.all_gather(x, axis, axis=0, tiled=False)  1630 us
    unnamed x5, waiting for transfers between devices  476 us
    psum x2, blocking collectives, on_device(): lax.psum(jnp.sum(live * conv_out, axis=0), everywhere) / live_count  212 us
    psum x2, blocking collectives, on_device(): lax.psum(jnp.sum(live * centred * centred, axis=0), everywhere) / live_count  201 us
    all_gather x1, waiting for transfers between devices, on_device(): weight_full = lax.all_gather(in_weight, 'tm', axis=0, tiled=True)  168 us
    psum x1, blocking collectives, on_device(): square_total = lax.psum(jnp.sum(direction * direction), 'tm')  132 us
  transfers between devices with their start and end apart: 10, of which 5 were waited for; matrix products, arithmetic and copies ran while one was open for 1% of the time, Pallas kernels for 0%

profile of v1, /device:TPU:2, one launch (start us, length us, event | category | flops | bytes accessed | tf_op | source)
XLA Modules:
  0.0 2971.6 jit_solution(10412478106846725645)
XLA Ops:
  7.2 0.7 all-gather.8.cloned.1.call-update
  7.9 1.2 dynamic_slice.7
  9.2 0.6 broadcast_select_fusion.1
  9.9 0.7 fusion.133
  10.5 1.8 slice_reduce_fusion.34
  12.5 1.4 fusion.121
  13.9 1.4 multiply_reduce_fusion.7
  15.4 1.2 broadcast_select_fusion
  16.5 168.4 %all-gather.8.cloned.1.call-done = bf16[3072,1536]{1,0:T(8,128)(2,1)} async-done(((bf16[48,1536]{1,0:T(8,128)(2,1)}), bf16[3072,1536]{1,0:T(8,128)(2,1)}) %all-gather.8.cloned.1.call-update) | async-done | bytes 9437200 | tf_op jit(solution)/shard_map/all_gather | solution.py:60
  184.9 7.2 fusion.122
  192.1 0.2 multiply_convert_fusion.3
  192.4 1.3 collective-permute-start.1
  193.7 3.0 collective-permute-start
  196.7 2.1 slice_reduce_fusion.33
  198.9 0.6 reduce_sum.723
  200.4 4.5 multiply_reduce_fusion.6
  204.9 104.2 %psum.42 = f32[1536]{0:T(1024)} all-reduce(f32[1536]{0:T(1024)} %get-tuple-element.124), channel_id=1, replica_groups=mesh['dp'=8,'tm'=64] {'dp','tm'}, use_global_device_ids=true, to_apply=%region_3.4 | all-reduce | flops 1536 | bytes 12288 | tf_op jit(solution)/shard_map/psum | solution.py:81
  309.1 0.7 broadcast_divide_fusion.1
  309.8 1.4 fusion.4
  311.2 99.4 %psum.43 = f32[1536]{0:T(1024)} all-reduce(f32[1536]{0:T(1024)} %fusion.4), channel_id=1, replica_groups=mesh['dp'=8,'tm'=64] {'dp','tm'}, use_global_device_ids=true, to_apply=%region_6.7 | all-reduce | flops 1536 | bytes 12288 | tf_op jit(solution)/shard_map/psum | solution.py:83
  410.6 0.7 add_rsqrt_fusion.1
  411.3 0.6 copy-done.63
  411.9 2.4 multiply_reduce_fusion.5
  414.3 0.6 maximum_bitcast_fusion
  415.0 817.2 %all-gather.10.cloned.1.call-done = f32[512,2,1536]{2,1,0:T(2,128)} async-done(((f32[1,2,1536]{2,1,0:T(2,128)}), f32[512,2,1536]{2,1,0:T(2,128)}) %all-gather.10.cloned.1.call-update) | async-done | bytes 6291472 | tf_op jit(solution)/shard_map/all_gather | solution.py:15
  1232.1 5.1 reduce_sum.727
  1237.2 0.8 slice_reduce_fusion.3
  1238.0 4.0 fusion.36
  1242.1 0.7 copy-done.2
  1242.8 1.3 collective-permute-start.3
  1244.1 3.2 collective-permute-start.2
  1248.1 1.3 maximum_convert_fusion.1
  1249.7 4.2 fusion
  1253.8 0.3 fusion.3
  1254.2 1.5 fusion.134
  1255.8 1.2 multiply_reduce_fusion.3
  1256.9 131.7 %psum.44 = f32[]{:T(128)} all-reduce(f32[]{:T(128)} %get-tuple-element.119), channel_id=1, replica_groups=mesh['dp'=8,'tm'=64] {'tm'}, use_global_device_ids=true, to_apply=%region_13.14 | all-reduce | flops 1 | bytes 8 | tf_op jit(solution)/shard_map/psum | solution.py:115
  1389.3 1.1 fusion.136
  1391.0 6.8 fusion.124
  1397.8 0.2 fusion.118
  1398.1 1.3 collective-permute-start.5
  1399.4 3.0 collective-permute-start.4
  1402.5 0.9 collective-permute-done.4
  1403.8 3.7 multiply_reduce_fusion.1
  1407.5 107.6 %psum.45 = f32[1536]{0:T(1024)} all-reduce(f32[1536]{0:T(1024)} %get-tuple-element.114), channel_id=1, replica_groups=mesh['dp'=8,'tm'=64] {'dp','tm'}, use_global_device_ids=true, to_apply=%region_48.49 | all-reduce | flops 1536 | bytes 12288 | tf_op jit(solution)/shard_map/psum | solution.py:81
  1515.1 0.7 broadcast_divide_fusion
  1515.8 1.4 fusion.5
  1517.2 101.4 %psum.46 = f32[1536]{0:T(1024)} all-reduce(f32[1536]{0:T(1024)} %fusion.5), channel_id=1, replica_groups=mesh['dp'=8,'tm'=64] {'dp','tm'}, use_global_device_ids=true, to_apply=%region_50.51 | all-reduce | flops 1536 | bytes 12288 | tf_op jit(solution)/shard_map/psum | solution.py:83
  1618.6 0.7 add_rsqrt_fusion
  1619.3 2.1 multiply_reduce_fusion
  1621.6 0.6 maximum_bitcast_fusion.1
  1622.2 0.3 all-reduce.4.cloned.1.call-start
  1622.5 1.2 fusion.35
  1629.2 809.0 %all-gather.12.cloned.1.call-done = f32[512,2,1536]{2,1,0:T(2,128)} async-done(((f32[1,2,1536]{2,1,0:T(2,128)}), f32[512,2,1536]{2,1,0:T(2,128)}) %all-gather.12.cloned.1.call-update) | async-done | bytes 6291472 | tf_op jit(solution)/shard_map/all_gather | solution.py:15
  2438.1 4.5 reduce_sum.768
  2442.7 2.3 fusion.67
  2445.1 1.2 fusion.66
  2451.7 0.9 copy.78
  2452.6 1.4 dynamic-slice
  2454.0 1.3 dynamic-slice_add_fusion
  2455.3 475.6 %all-reduce.4.cloned.1.call-done = f32[64,6,128]{2,1,0:T(8,128)} async-done(((f32[64,6,128]{2,1,0:T(8,128)}), f32[64,6,128]{2,1,0:T(8,128)}) %all-reduce.4.cloned.1.call-update) | async-done | bytes 196624
  2930.9 1.4 constant_dynamic-slice_fusion
  2932.4 32.0 %psum.47 = f32[32,24]{1,0:T(8,128)S(1)} all-reduce(f32[32,24]{1,0:T(8,128)S(1)} %slice.682), channel_id=1, replica_groups=mesh['dp'=8,'tm'=64] {'dp'}, use_global_device_ids=true, to_apply=%region_86.87 | all-reduce | flops 768 | bytes 6144 | tf_op jit(solution)/shard_map/psum | solution.py:125
  2964.4 0.7 copy.77
  (406 shorter events, 11.2 us)
Async XLA Ops:
  7.2 177.7 %all-gather.8.cloned.1.call-start = ((), (), s32[]{:S(2)}) async-start(), calls=%async_computation | async-start | bytes 9584640 | tf_op jit(solution)/shard_map/all_gather | solution.py:60
  7.9 1224.2 %all-gather.10.cloned.1.call-start = ((), (), s32[]{:S(2)}) async-start(), calls=%async_computation.1 | async-start | bytes 6303744 | tf_op jit(solution)/shard_map/all_gather | solution.py:15
  9.8 182.2 %copy-start.85 = (f32[128]{0:T(128)}, f32[128]{0:T(128)S(1)}, u32[]{:S(2)}) copy-start(f32[128]{0:T(128)S(1)} %broadcast_select_fusion.1) | copy-start | bytes 1540
  10.5 181.6 %copy-start.64 = (f32[128]{0:T(128)}, f32[128]{0:T(128)S(1)}, u32[]{:S(2)}) copy-start(f32[128]{0:T(128)S(1)} %fusion.133) | copy-start | bytes 1540
  12.3 1237.0 %copy-start.7 = (f32[1536]{0:T(1024)}, f32[1536]{0:T(1024)S(1)}, u32[]{:S(2)}) copy-start(f32[1536]{0:T(1024)S(1)} %get-tuple-element.78) | copy-start | bytes 18436
  12.4 1237.0 %copy-start.9 = (f32[1536]{0:T(1024)}, f32[1536]{0:T(1024)S(1)}, u32[]{:S(2)}) copy-start(f32[1536]{0:T(1024)S(1)} %get-tuple-element.79) | copy-start | bytes 18436
  12.4 1237.0 %copy-start.11 = (f32[1536]{0:T(1024)}, f32[1536]{0:T(1024)S(1)}, u32[]{:S(2)}) copy-start(f32[1536]{0:T(1024)S(1)} %get-tuple-element.80) | copy-start | bytes 18436
  12.4 1237.0 %copy-start.13 = (f32[1536]{0:T(1024)}, f32[1536]{0:T(1024)S(1)}, u32[]{:S(2)}) copy-start(f32[1536]{0:T(1024)S(1)} %get-tuple-element.81) | copy-start | bytes 18436
  12.4 1237.0 %copy-start.15 = (f32[1536]{0:T(1024)}, f32[1536]{0:T(1024)S(1)}, u32[]{:S(2)}) copy-start(f32[1536]{0:T(1024)S(1)} %get-tuple-element.82) | copy-start | bytes 18436
  12.4 1237.0 %copy-start.17 = (f32[1536]{0:T(1024)}, f32[1536]{0:T(1024)S(1)}, u32[]{:S(2)}) copy-start(f32[1536]{0:T(1024)S(1)} %get-tuple-element.83) | copy-start | bytes 18436
  12.4 1237.0 %copy-start.19 = (f32[1536]{0:T(1024)}, f32[1536]{0:T(1024)S(1)}, u32[]{:S(2)}) copy-start(f32[1536]{0:T(1024)S(1)} %get-tuple-element.84) | copy-start | bytes 18436
  12.4 1237.0 %copy-start.21 = (f32[1536]{0:T(1024)}, f32[1536]{0:T(1024)S(1)}, u32[]{:S(2)}) copy-start(f32[1536]{0:T(1024)S(1)} %get-tuple-element.85) | copy-start | bytes 18436
  12.4 1237.0 %copy-start.23 = (f32[1536]{0:T(1024)}, f32[1536]{0:T(1024)S(1)}, u32[]{:S(2)}) copy-start(f32[1536]{0:T(1024)S(1)} %get-tuple-element.86) | copy-start | bytes 18436
  12.4 1237.0 %copy-start.25 = (f32[1536]{0:T(1024)}, f32[1536]{0:T(1024)S(1)}, u32[]{:S(2)}) copy-start(f32[1536]{0:T(1024)S(1)} %get-tuple-element.87) | copy-start | bytes 18436
  12.4 1237.0 %copy-start.27 = (f32[1536]{0:T(1024)}, f32[1536]{0:T(1024)S(1)}, u32[]{:S(2)}) copy-start(f32[1536]{0:T(1024)S(1)} %get-tuple-element.88) | copy-start | bytes 18436
  12.5 1237.0 %copy-start.29 = (f32[1536]{0:T(1024)}, f32[1536]{0:T(1024)S(1)}, u32[]{:S(2)}) copy-start(f32[1536]{0:T(1024)S(1)} %get-tuple-element.89) | copy-start | bytes 18436
  12.5 1237.0 %copy-start.31 = (f32[1536]{0:T(1024)}, f32[1536]{0:T(1024)S(1)}, u32[]{:S(2)}) copy-start(f32[1536]{0:T(1024)S(1)} %get-tuple-element.90) | copy-start | bytes 18436
  12.5 1237.0 %copy-start.33 = (f32[1536]{0:T(1024)}, f32[1536]{0:T(1024)S(1)}, u32[]{:S(2)}) copy-start(f32[1536]{0:T(1024)S(1)} %get-tuple-element.91) | copy-start | bytes 18436
  12.5 1237.0 %copy-start.35 = (f32[1536]{0:T(1024)}, f32[1536]{0:T(1024)S(1)}, u32[]{:S(2)}) copy-start(f32[1536]{0:T(1024)S(1)} %get-tuple-element.92) | copy-start | bytes 18436
  12.5 1237.0 %copy-start.37 = (f32[1536]{0:T(1024)}, f32[1536]{0:T(1024)S(1)}, u32[]{:S(2)}) copy-start(f32[1536]{0:T(1024)S(1)} %get-tuple-element.93) | copy-start | bytes 18436
  12.5 1237.0 %copy-start.39 = (f32[1536]{0:T(1024)}, f32[1536]{0:T(1024)S(1)}, u32[]{:S(2)}) copy-start(f32[1536]{0:T(1024)S(1)} %get-tuple-element.94) | copy-start | bytes 18436
  12.5 1237.0 %copy-start.41 = (f32[1536]{0:T(1024)}, f32[1536]{0:T(1024)S(1)}, u32[]{:S(2)}) copy-start(f32[1536]{0:T(1024)S(1)} %get-tuple-element.95) | copy-start | bytes 18436
  13.9 178.2 %copy-start.89 = (f32[128]{0:T(128)}, f32[128]{0:T(128)S(1)}, u32[]{:S(2)}) copy-start(f32[128]{0:T(128)S(1)} %broadcast_multiply_fusion.3) | copy-start | bytes 1540
  16.5 175.8 %copy-start.87 = (f32[128]{0:T(128)}, f32[128]{0:T(128)S(1)}, u32[]{:S(2)}) copy-start(f32[128]{0:T(128)S(1)} %get-tuple-element.134) | copy-start | bytes 1540
  184.9 14.0 copy-start.92
  192.4 7.8 collective-permute-start.1
  193.7 6.5 collective-permute-start
  198.9 1050.7 %copy-start.43 = (f32[1536]{0:T(1024)}, f32[1536]{0:T(1024)S(1)}, u32[]{:S(2)}) copy-start(f32[1536]{0:T(1024)S(1)} %get-tuple-element.96) | copy-start | bytes 18436
  198.9 1050.7 %copy-start.45 = (f32[1536]{0:T(1024)}, f32[1536]{0:T(1024)S(1)}, u32[]{:S(2)}) copy-start(f32[1536]{0:T(1024)S(1)} %get-tuple-element.97) | copy-start | bytes 18436
  198.9 1050.7 %copy-start.47 = (f32[1536]{0:T(1024)}, f32[1536]{0:T(1024)S(1)}, u32[]{:S(2)}) copy-start(f32[1536]{0:T(1024)S(1)} %get-tuple-element.98) | copy-start | bytes 18436
  198.9 1050.7 %copy-start.49 = (f32[1536]{0:T(1024)}, f32[1536]{0:T(1024)S(1)}, u32[]{:S(2)}) copy-start(f32[1536]{0:T(1024)S(1)} %get-tuple-element.99) | copy-start | bytes 18436
  198.9 1050.7 %copy-start.51 = (f32[1536]{0:T(1024)}, f32[1536]{0:T(1024)S(1)}, u32[]{:S(2)}) copy-start(f32[1536]{0:T(1024)S(1)} %get-tuple-element.100) | copy-start | bytes 18436
  200.3 211.5 %copy-start.6 = (f32[1536]{0:T(1024)S(1)}, f32[1536]{0:T(1024)}, u32[]{:S(2)}) copy-start(f32[1536]{0:T(1024)} %param.13) | copy-start | bytes 18436
  414.9 2023.2 %all-gather.12.cloned.1.call-start = ((), (), s32[]{:S(2)}) async-start(), calls=%async_computation.2 | async-start | bytes 6303744 | tf_op jit(solution)/shard_map/all_gather | solution.py:15
  1242.8 5.2 collective-permute-start.3
  1244.1 3.9 collective-permute-start.2
  1390.7 12.7 copy-start.8
  1390.7 12.7 copy-start.10
  1390.7 12.7 copy-start.12
  1390.7 12.7 copy-start.14
  1390.7 12.7 copy-start.16
  1390.7 12.7 copy-start.18
  1390.8 12.7 copy-start.20
  1390.8 12.7 copy-start.22
  1390.8 12.7 copy-start.24
  1390.8 12.7 copy-start.26
  1390.8 12.7 copy-start.28
  1390.8 12.7 copy-start.30
  1390.8 12.7 copy-start.32
  1390.8 12.7 copy-start.34
  1390.8 12.7 copy-start.36
  1390.8 12.7 copy-start.38
  1390.9 12.7 copy-start.40
  1390.9 12.7 copy-start.42
  1390.9 12.7 copy-start.44
  1390.9 12.7 copy-start.46
  1398.1 4.3 collective-permute-start.5
  1399.4 3.9 collective-permute-start.4
  1403.7 215.6 %copy-start.5 = (bf16[1,128,1536]{2,1,0:T(8,128)(2,1)S(1)}, bf16[1,128,1536]{2,1,0:T(8,128)(2,1)}, u32[]{:S(2)}) copy-start(bf16[1,128,1536]{2,1,0:T(8,128)(2,1)} %param.10) | copy-start | bytes 1179652
  1403.8 218.8 %copy-start.3 = (bf16[128,1536]{1,0:T(8,128)(2,1)S(1)}, bf16[128,1536]{1,0:T(8,128)(2,1)}, u32[]{:S(2)}) copy-start(bf16[128,1536]{1,0:T(8,128)(2,1)} %copy-done.2) | copy-start | bytes 1179652
  1622.2 1308.7 %all-reduce.4.cloned.1.call-start = ((), (), s32[]{:S(2)}) async-start(), calls=%async_computation.3 | async-start | bytes 524288
  1623.7 819.0 %copy-start.4 = (f32[128,1536]{1,0:T(8,128)S(1)}, f32[128,1536]{1,0:T(8,128)}, u32[]{:S(2)}) copy-start(f32[128,1536]{1,0:T(8,128)} %get-tuple-element.113) | copy-start | bytes 2359300
  1623.7 819.0 %copy-start.62 = (f32[1536]{0:T(1024)S(1)}, f32[1536]{0:T(1024)}, u32[]{:S(2)}) copy-start(f32[1536]{0:T(1024)} %copy-done.61) | copy-start | bytes 18436
  1623.7 819.0 %copy-start.66 = (f32[128]{0:T(128)S(1)}, f32[128]{0:T(128)}, u32[]{:S(2)}) copy-start(f32[128]{0:T(128)} %copy-done.64) | copy-start | bytes 1540
  (42 other events, 253.6 us)
Sparse Core Ops, SparseCore 0:
  11.3 173.5 all-gather.7
  415.0 817.0 all-gather.9
  1622.3 815.7 all-gather.11
  2452.7 478.1 all-reduce.3
